TPU v7x, 256 devices: a whole 4x4x8 slice. The times are simulated.
256 devices in a mesh: dp: 64 (over z_hi, y, x), mp: 4 (over z_lo, core).
Axes of the slice: x: 4, y: 4, z: 8 (z_hi: 4, z_lo: 2; z = z_hi * 2 + z_lo), core: 2. Of those that a mesh axis runs over, the one named last changes fastest.
Arguments:
- hidden: bfloat16 [2048, 16, 2048], P('dp', None, 'mp'), may hold values from -6 to 6
- norm_gain: bfloat16 [2048], P('mp'), may hold values from 0.099609375 to 1.8984375
- in_x: bfloat16 [2048, 4096], P('dp', 'mp'), may hold values from -0.125 to 0.125
- in_z: bfloat16 [2048, 4096], P('dp', 'mp'), may hold values from -0.125 to 0.125
- conv_weight: float32 [4, 4096], P(None, 'mp'), may hold values from -3 to 3
- conv_bias: float32 [4096], P('mp'), may hold values from -3 to 3
- x_proj: bfloat16 [4096, 160], P(('mp', 'dp')), may hold values from -0.09375 to 0.09375
- dt_proj: bfloat16 [128, 4096], P('dp', 'mp'), may hold values from -0.5 to 0.5
- dt_bias: float32 [4096], P('mp'), may hold values from -5 to -1
- a_log: float32 [16, 4096], P(None, 'mp'), may hold values from 0 to 2.77
- skip: float32 [4096], P('mp'), may hold values from 0.5 to 1.5
- out_proj: bfloat16 [4096, 2048], P('mp', 'dp'), may hold values from -0.09375 to 0.09375
- state_pool: float32 [2560, 16, 4096], P('dp', None, 'mp'), may hold values from -6 to 6
- conv_pool: float32 [2560, 3, 4096], P('dp', None, 'mp'), may hold values from -6 to 6
- permutation: int32 [2048], P('dp'), may hold values from 0 to 2047, as said below
- page_table: int32 [2048], P('dp'), may hold values from 0 to 2559, as said below
- accepted: int32 [2048], P('dp'), may hold values from 1 to 16
Outputs:
- verified: bfloat16 [2048, 16, 2048], P('dp', None, 'mp')
- new_state_pool: float32 [2560, 16, 4096], P('dp', None, 'mp')
- new_conv_pool: float32 [2560, 3, 4096], P('dp', None, 'mp')
Inputs may be any that keep to these rules, and one draw needn't show every extreme that they name: `permutation`: A request at position j of the block of dp index d goes to position j of the block of dp index (d + o) mod 64, where the shift o depends only on j mod 32 and takes 32 different values; so each dp index sends exactly 1 request to each of 32 dp indices and receives 32. `page_table`: the requests of dp index d use distinct slots among the 40 slots d * 40 .. (d + 1) * 40 - 1.
All inputs are finite; a program needn't handle non-finite values.
Results may differ from a plain program's by a relative error of at most 0.0065.
Values may be sent and summed in bfloat16 or wider, within the bound.
No kernel may reach another device: no remote copies, remote signals or barrier semaphores. Data moves between devices by JAX's collectives and lax.ppermute only.
A program may use at most 128 MiB of HBM per device.

v0:
```python
import jax
import jax.numpy as jnp
from jax import lax
from jax.sharding import PartitionSpec as P

EPS = 1e-05


def route_plan(permutation, count, peers):
    capacity = count // min(count, peers)
    target = permutation // count
    order = jnp.arange(count)
    earlier = (target[:, None] == target[None, :]) & (order[None, :] < order[:, None])
    rank_within = jnp.sum(earlier.astype(jnp.int32), axis=1)
    position = target * capacity + rank_within
    match = position[None, :] == jnp.arange(peers * capacity)[:, None]
    filled = jnp.any(match, axis=1)
    source = jnp.argmax(match, axis=1)
    return (position, filled, source)


def pack_rows(values, filled, source):
    picked = jnp.take(values, source, axis=0)
    shape = (filled.shape[0],) + (1,) * (values.ndim - 1)
    return jnp.where(filled.reshape(shape), picked, jnp.zeros_like(picked))


def unpack_rows(values, arrived, count):
    match = arrived[None, :] == jnp.arange(count)[:, None]
    index = jnp.argmax(match, axis=1)
    return jnp.take(values, index, axis=0)


def write_pool(pool, slot_local, values):
    match = slot_local[None, :] == jnp.arange(pool.shape[0])[:, None]
    filled = jnp.any(match, axis=1)
    index = jnp.argmax(match, axis=1)
    return jnp.where(filled[:, None, None], jnp.take(values, index, axis=0), pool)


def verify_layer(
    hidden,
    norm_gain,
    in_x,
    in_z,
    conv_weight,
    conv_bias,
    x_proj,
    dt_proj,
    dt_bias,
    a_log,
    skip,
    out_proj,
    caches,
    accepted,
):
    count, drafts, width_local = hidden.shape
    tokens = count * drafts
    inner_local = in_x.shape[1]
    state_count = a_log.shape[0]
    taps = conv_weight.shape[0]
    rank = x_proj.shape[1] - 2 * state_count
    full, gain_full = (
        lax.all_gather(hidden, "mp", axis=2, tiled=True),
        lax.all_gather(norm_gain, "mp", axis=0, tiled=True),
    )
    rows = full.reshape(tokens, -1).astype(jnp.float32)
    scale = lax.rsqrt(jnp.mean(rows * rows, axis=1, keepdims=True) + EPS)
    normed = (rows * scale * gain_full.astype(jnp.float32)).astype(jnp.bfloat16)
    columns = normed
    x_wide = jnp.dot(
        columns, lax.all_gather(in_x, "dp", axis=0, tiled=True), preferred_element_type=jnp.float32
    )
    z_wide = jnp.dot(
        columns, lax.all_gather(in_z, "dp", axis=0, tiled=True), preferred_element_type=jnp.float32
    )
    x_part = x_wide.astype(jnp.bfloat16)
    z_part = z_wide.astype(jnp.bfloat16)
    states = caches[:, :state_count, :]
    edges = caches[:, state_count:, :]
    padded = jnp.concatenate(
        [edges, x_part.astype(jnp.float32).reshape(count, drafts, inner_local)], axis=1
    )
    mixed = conv_bias + jnp.zeros((count, drafts, inner_local), jnp.float32)
    for offset in range(taps):
        mixed = mixed + conv_weight[offset] * padded[:, offset : offset + drafts, :]
    inputs = jax.nn.silu(mixed).astype(jnp.bfloat16)
    flat_inputs = inputs.reshape(tokens, inner_local)
    piece = lax.all_gather(x_proj, "dp", axis=0, tiled=True)
    columns = flat_inputs
    low_sum = jnp.dot(columns, piece[:, :rank], preferred_element_type=jnp.float32)
    both_sum = jnp.einsum("ks,tk->st", piece[:, rank:], columns, preferred_element_type=jnp.float32)
    low_full, both = lax.psum((low_sum, both_sum), "mp")
    low_half = low_full.astype(jnp.bfloat16)
    columns = low_half
    delta = jnp.dot(
        columns,
        lax.all_gather(dt_proj, "dp", axis=0, tiled=True),
        preferred_element_type=jnp.float32,
    )
    delta = jax.nn.softplus(delta + dt_bias).reshape(count, drafts, inner_local)
    decay_rate = -jnp.exp(a_log)
    inputs_wide = inputs.astype(jnp.float32)
    driven = delta * inputs_wide
    b_time = both[:state_count].reshape(state_count, count, drafts).transpose(2, 1, 0)
    c_time = both[state_count:].reshape(state_count, count, drafts).transpose(2, 1, 0)

    def advance(carry, slices):
        state, kept = carry
        step_delta, step_drive, step_b, step_c, index = slices
        state = (
            jnp.exp(step_delta[:, None, :] * decay_rate[None]) * state
            + step_drive[:, None, :] * step_b[:, :, None]
        )
        output = jnp.sum(state * step_c[:, :, None], axis=1)
        kept = jnp.where((accepted - 1 == index)[:, None, None], state, kept)
        return ((state, kept), output)

    (final_state, kept), outputs = lax.scan(
        advance,
        (states, states),
        (
            delta.transpose(1, 0, 2),
            driven.transpose(1, 0, 2),
            b_time,
            c_time,
            jnp.arange(drafts, dtype=jnp.int32),
        ),
    )
    outputs = outputs.transpose(1, 0, 2)
    gate_wide = z_part.astype(jnp.float32).reshape(count, drafts, inner_local)
    gated = (
        ((outputs + skip * inputs_wide) * jax.nn.silu(gate_wide))
        .astype(jnp.bfloat16)
        .reshape(tokens, inner_local)
    )
    index = accepted[:, None] + jnp.arange(taps - 1, dtype=jnp.int32)[None, :]
    new_edges = jnp.take_along_axis(padded, index[:, :, None], axis=1)
    new_caches = jnp.concatenate([kept, new_edges], axis=1)
    terms = jnp.dot(
        gated,
        lax.all_gather(out_proj, "dp", axis=1, tiled=True),
        preferred_element_type=jnp.float32,
    )
    summed = lax.psum_scatter(terms, "mp", scatter_dimension=1, tiled=True)
    result = (summed + hidden.reshape(tokens, width_local).astype(jnp.float32)).astype(jnp.bfloat16)
    return (result.reshape(count, drafts, width_local), new_caches)


def on_device(
    hidden,
    norm_gain,
    in_x,
    in_z,
    conv_weight,
    conv_bias,
    x_proj,
    dt_proj,
    dt_bias,
    a_log,
    skip,
    out_proj,
    state_pool,
    conv_pool,
    permutation,
    page_table,
    accepted,
):
    count = hidden.shape[0]
    state_count = state_pool.shape[1]
    pool_count = state_pool.shape[0]
    peers = lax.axis_size("dp")
    slot_local = page_table % pool_count
    caches = jnp.concatenate(
        [jnp.take(state_pool, slot_local, axis=0), jnp.take(conv_pool, slot_local, axis=0)], axis=1
    )
    position, filled, source = route_plan(permutation, count, peers)
    arrival_slot = permutation % count
    details = jnp.stack([arrival_slot, accepted], axis=1).astype(jnp.float32)
    details_sent = jnp.where(filled[:, None], jnp.take(details, source, axis=0), -1.0)
    got_hidden = lax.all_to_all(
        pack_rows(hidden, filled, source), "dp", split_axis=0, concat_axis=0, tiled=True
    )
    got_caches, got_details = (
        lax.all_to_all(
            pack_rows(caches, filled, source), "dp", split_axis=0, concat_axis=0, tiled=True
        ),
        lax.all_to_all(details_sent, "dp", split_axis=0, concat_axis=0, tiled=True),
    )
    arrived = got_details[:, 0].astype(jnp.int32)
    local_hidden = unpack_rows(got_hidden, arrived, count)
    local_caches = unpack_rows(got_caches, arrived, count)
    local_accept = unpack_rows(got_details[:, 1], arrived, count).astype(jnp.int32)
    verified, new_caches = verify_layer(
        local_hidden,
        norm_gain,
        in_x,
        in_z,
        conv_weight,
        conv_bias,
        x_proj,
        dt_proj,
        dt_bias,
        a_log,
        skip,
        out_proj,
        local_caches,
        local_accept,
    )
    returned = jnp.take(new_caches, jnp.maximum(arrived, 0), axis=0)
    returned = jnp.where((arrived >= 0)[:, None, None], returned, jnp.zeros_like(returned))
    back = lax.all_to_all(
        returned.astype(jnp.bfloat16), "dp", split_axis=0, concat_axis=0, tiled=True
    ).astype(returned.dtype)
    settled = jnp.take(back, position, axis=0)
    new_state_pool = write_pool(state_pool, slot_local, settled[:, :state_count])
    new_conv_pool = write_pool(conv_pool, slot_local, settled[:, state_count:])
    return (verified, new_state_pool, new_conv_pool)


def solution(mesh):
    return jax.shard_map(
        on_device,
        mesh=mesh,
        in_specs=(
            P("dp", None, "mp"),
            P("mp"),
            P("dp", "mp"),
            P("dp", "mp"),
            P(None, "mp"),
            P("mp"),
            P(("mp", "dp"), None),
            P("dp", "mp"),
            P("mp"),
            P(None, "mp"),
            P("mp"),
            P("mp", "dp"),
            P("dp", None, "mp"),
            P("dp", None, "mp"),
            P("dp"),
            P("dp"),
            P("dp"),
        ),
        out_specs=(P("dp", None, "mp"), P("dp", None, "mp"), P("dp", None, "mp")),
        check_vma=False,
    )
```

profile of v0, /device:TPU:1, one launch (start us, length us, event | category | flops | bytes accessed | tf_op | source)
XLA Modules:
  0.0 935.4 jit_solution(18091020469888556631)
XLA Ops:
  11.0 15.1 %all-to-all-start.1 = ((f32[64,1,2]{2,1,0:T(1,128)}), f32[64,1,2]{2,1,0:T(1,128)S(1)}, u32[]{:S(2)}, u32[]{:S(2)}) async-start(f32[64,1,2]{2,1,0:T(1,128)} %copy.94), calls=%async_computation.1 | async-start | bytes 65536 | tf_op jit(solution)/shard_map/all_to_all | solution.py:188
  27.9 8.8 all-to-all-done.1
  36.7 5.5 all-to-all-start.2
  43.8 23.7 %all-to-all-done.2 = bf16[64,16,512]{2,1,0:T(8,128)(2,1)} async-done(((bf16[64,16,512]{2,1,0:T(8,128)(2,1)}), bf16[64,16,512]{2,1,0:T(8,128)(2,1)}, u32[]{:S(2)}, u32[]{:S(2)}) %all-to-all-start.2) | async-done | bytes 1048608 | tf_op jit(solution)/shard_map/all_to_all | solution.py:181
  67.5 2.6 gather_fusion.4
  77.5 3.6 gather_fusion.9
  81.1 7.0 select_select_fusion.1
  88.2 10.0 %all-to-all-start = ((f32[64,19,1024]{2,1,0:T(8,128)}), f32[64,19,1024]{2,1,0:T(8,128)}, u32[]{:S(2)}, u32[]{:S(2)}) async-start(f32[64,19,1024]{2,1,0:T(8,128)} %select_select_fusion.1), calls=%async_computation | async-start | bytes 12582912 | tf_op jit(solution)/shard_map/all_to_all | solution.py:185
  99.0 141.4 %all-gather = bf16[4,1,512]{2,1,0:T(2,128)(2,1)S(1)} all-gather(bf16[1,1,512]{2,1,0:T(2,128)(2,1)S(1)} %reshape.371), channel_id=1, replica_groups=mesh['dp'=64,'mp'=4] {'mp'}, dimensions={0}, use_global_device_ids=true | all-gather | bytes 5120 | tf_op jit(solution)/shard_map/all_gather | solution.py:65
  240.4 184.1 %all_gather.24 = bf16[1024,160]{1,0:T(8,128)(2,1)} all-gather(bf16[16,160]{1,0:T(8,128)(2,1)S(1)} %copy-done.16), channel_id=1, replica_groups=mesh['dp'=64,'mp'=4] {'dp'}, dimensions={0}, use_global_device_ids=true | all-gather | bytes 332800 | tf_op jit(solution)/shard_map/all_gather | solution.py:89
  428.8 5.2 convolution_convert_fusion.1
  434.2 5.2 gather_fusion.10
  439.5 2.3 broadcast_select_fusion.2
  444.9 2.6 multiply_convert_fusion
  451.2 160.2 %all-gather.1 = bf16[64,2,1024]{2,1,0:T(2,128)(2,1)S(1)} all-gather(bf16[1,2,1024]{2,1,0:T(2,128)(2,1)S(1)} %bitcast.97), channel_id=1, replica_groups=mesh['dp'=64,'mp'=4] {'dp'}, dimensions={0}, use_global_device_ids=true | all-gather | bytes 266240 | tf_op jit(solution)/shard_map/all_gather | solution.py:98
  612.2 4.5 convolution_convert_fusion
  619.9 68.9 %all-reduce.4 = bf16[512,128]{1,0:T(8,128)(2,1)} all-reduce(f32[512,128]{1,0:T(8,128)S(1)} %fusion.12), channel_id=1, replica_groups=mesh['dp'=64,'mp'=4] {'mp'}, use_global_device_ids=true, to_apply=%region_5.8 | all-reduce | flops 65536 | bytes 393216 | tf_op jit(solution)/shard_map/psum | solution.py:93
  688.8 2.3 compare_select_fusion
  691.1 4.6 fusion.3
  698.7 82.8 %while.16 = (s32[]{:T(128)}, f32[32,16,1024]{2,1,0:T(8,128)S(1)}, bf16[32,16,1024]{2,1,0:T(8,128)(2,1)S(1)}, f32[16,32,1024]{2,1,0:T(8,128)}, f32[16,32,1024]{2,...) while((s32[]{:T(128)}, f32[32,16,1024]{2,1,0:T(8,128)S(1)}, ...), condition=%wide.region_9.12_spmd, body=%wide.region_7.11_spmd.sunk | while | flops 3637314 | bytes 9646925 | solution.py:119
  781.5 4.1 fusion.6
  786.3 6.6 fusion.29
  794.4 3.3 gather_fusion.8
  798.5 2.4 gather_fusion.11
  800.8 5.5 fusion
  806.4 5.1 all-to-all-start.3
  811.8 94.2 %all-to-all-done.3 = bf16[64,19,1024]{2,1,0:T(8,128)(2,1)S(1)} async-done(((bf16[64,19,1024]{2,1,0:T(8,128)(2,1)}), bf16[64,19,1024]{2,1,0:T(8,128)(2,1)S(1)}, u32[]{:S(2)}, u32[]{:S(2)}) %all-to-all-start.3) | async-done | bytes 2490400 | tf_op jit(solution)/shard_map/all_to_all | solution.py:212
  905.9 3.4 convert_element_type.91
  909.3 3.5 gather_fusion.12
  916.7 3.0 gather_fusion.7
  922.3 3.7 select_select_fusion.2
  926.0 2.3 add_convert_fusion
  (268 shorter events, 125.0 us)
Async XLA Ops:
  7.2 18.9 %copy-start = (bf16[32,16,512]{2,1,0:T(8,128)(2,1)S(1)}, bf16[32,16,512]{2,1,0:T(8,128)(2,1)}, u32[]{:S(2)}) copy-start(bf16[32,16,512]{2,1,0:T(8,128)(2,1)} %param.23) | copy-start | bytes 1572868
  8.1 19.8 %copy-start.21 = (s32[32]{0:T(128)}, s32[32]{0:T(128)S(1)}, u32[]{:S(2)}) copy-start(s32[32]{0:T(128)S(1)} %get-tuple-element.243) | copy-start | bytes 388
  11.0 25.8 %all-to-all-start.1 = ((f32[64,1,2]{2,1,0:T(1,128)}), f32[64,1,2]{2,1,0:T(1,128)S(1)}, u32[]{:S(2)}, u32[]{:S(2)}) async-start(f32[64,1,2]{2,1,0:T(1,128)} %copy.94), calls=%async_computation.1 | async-start | bytes 65536 | tf_op jit(solution)/shard_map/all_to_all | solution.py:188
  36.7 30.7 %all-to-all-start.2 = ((bf16[64,16,512]{2,1,0:T(8,128)(2,1)}), bf16[64,16,512]{2,1,0:T(8,128)(2,1)}, u32[]{:S(2)}, u32[]{:S(2)}) async-start(bf16[64,16,512]{2,1,0:T(8,128)(2,1)} %select_select_fusion.3), calls=%async_computation.2 | async-start | bytes 2097152 | tf_op jit(solution)/shard_map/all_to_all | solution.py:181
  42.3 30.6 %copy-start.24 = (s32[32]{0:T(128)S(1)}, s32[32]{0:T(128)}, u32[]{:S(2)}) copy-start(s32[32]{0:T(128)} %param.38) | copy-start | bytes 388
  42.3 31.1 %copy-start.8 = (f32[40,16,1024]{2,1,0:T(8,128)S(1)}, f32[40,16,1024]{2,1,0:T(8,128)}, u32[]{:S(2)}) copy-start(f32[40,16,1024]{2,1,0:T(8,128)} %param.35) | copy-start | bytes 7864324
  42.3 382.3 %all-gather.7.cloned.1.call-start = ((), (), s32[]{:S(2)}) async-start(), calls=%async_computation.5 | async-start | bytes 2621440 | tf_op jit(solution)/shard_map/all_gather | solution.py:64
  72.1 356.7 %all-gather.9.cloned.1.call-start = ((), (), s32[]{:S(2)}) async-start(), calls=%async_computation.6 | async-start | bytes 4259840 | tf_op jit(solution)/shard_map/all_gather | solution.py:72
  73.4 2.0 copy-start.2
  88.2 10.8 %copy-start.20 = (bf16[512]{0:T(512)(128)(2,1)S(1)}, bf16[512]{0:T(512)(128)(2,1)}, u32[]{:S(2)}) copy-start(bf16[512]{0:T(512)(128)(2,1)} %param.24) | copy-start | bytes 3076
  88.2 152.3 %copy-start.16 = (bf16[16,160]{1,0:T(8,128)(2,1)S(1)}, bf16[16,160]{1,0:T(8,128)(2,1)}, u32[]{:S(2)}) copy-start(bf16[16,160]{1,0:T(8,128)(2,1)} %param.29) | copy-start | bytes 15364
  88.2 336.4 %copy-start.15 = (f32[4,1024]{1,0:T(4,128)S(1)}, f32[4,1024]{1,0:T(4,128)}, u32[]{:S(2)}) copy-start(f32[4,1024]{1,0:T(4,128)} %param.27) | copy-start | bytes 49156
  88.2 346.0 %all-to-all-start = ((f32[64,19,1024]{2,1,0:T(8,128)}), f32[64,19,1024]{2,1,0:T(8,128)}, u32[]{:S(2)}, u32[]{:S(2)}) async-start(f32[64,19,1024]{2,1,0:T(8,128)} %select_select_fusion.1), calls=%async_computation | async-start | bytes 12582912 | tf_op jit(solution)/shard_map/all_to_all | solution.py:185
  98.2 514.0 %all-gather.11.cloned.1.call-start = ((), (), s32[]{:S(2)}) async-start(), calls=%async_computation.8 | async-start | bytes 4259840 | tf_op jit(solution)/shard_map/all_gather | solution.py:75
  98.9 596.8 %all-reduce.3.cloned.1.call-start = ((), (), s32[]{:S(2)}) async-start(), calls=%async_computation.7 | async-start | bytes 131072 | tf_op jit(solution)/shard_map/psum | solution.py:93
  424.6 2.3 copy-start.9
  441.7 1.7 copy-start.5
  442.1 2.8 copy-start.17
  444.9 4.6 copy-start.12
  447.5 3.7 copy-start.18
  447.5 164.7 %copy-start.14 = (f32[16,1024]{1,0:T(8,128)S(1)}, f32[16,1024]{1,0:T(8,128)}, u32[]{:S(2)}) copy-start(f32[16,1024]{1,0:T(8,128)} %param.32) | copy-start | bytes 196612
  447.5 164.7 %copy-start.11 = (bf16[512,2048]{1,0:T(8,128)(2,1)S(1)}, bf16[512,2048]{1,0:T(8,128)(2,1)}, u32[]{:S(2)}) copy-start(bf16[512,2048]{1,0:T(8,128)(2,1)} %fusion.2) | copy-start | bytes 6291460
  450.5 335.8 %all-gather.13.cloned.1.call-start = ((), (), s32[]{:S(2)}) async-start(), calls=%async_computation.9 | async-start | bytes 4259840 | tf_op jit(solution)/shard_map/all_gather | solution.py:142
  451.1 474.9 %reduce-scatter.2.cloned.1.call-start = ((), (), s32[]{:S(2)}) async-start(), calls=%async_computation.10 | async-start | bytes 5242880 | tf_op jit(solution)/shard_map/reduce_scatter | solution.py:145
  616.8 2.8 copy-start.6
  619.6 69.2 %copy-start.23 = (f32[1024]{0:T(1024)S(1)}, f32[1024]{0:T(1024)}, u32[]{:S(2)}) copy-start(f32[1024]{0:T(1024)} %param.31) | copy-start | bytes 12292
  698.7 82.8 %copy-start.19 = (f32[1024]{0:T(1024)S(1)}, f32[1024]{0:T(1024)}, u32[]{:S(2)}) copy-start(f32[1024]{0:T(1024)} %param.33) | copy-start | bytes 12292
  806.4 5.1 copy-start.22
  806.4 99.6 %all-to-all-start.3 = ((bf16[64,19,1024]{2,1,0:T(8,128)(2,1)}), bf16[64,19,1024]{2,1,0:T(8,128)(2,1)S(1)}, u32[]{:S(2)}, u32[]{:S(2)}) async-start(bf16[64,19,1024]{2,1,0:T(8,128)(2,1)} %fusion), calls=%async_computation.4 | async-start | bytes 6291456 | tf_op jit(solution)/shard_map/all_to_all | solution.py:212
  914.5 5.2 copy-start.3
  916.7 5.6 copy-start.7
  922.3 6.0 copy-start.1
  (5 other events, 5.8 us)
Sparse Core Ops, SparseCore 0:
  72.2 72.1 all-gather.6
  147.7 163.9 all-gather.8
  315.0 87.4 all-gather.10
  450.6 61.1 all-reduce.2
  515.5 88.7 all-gather.12
  793.0 89.7 reduce-scatter.1
where the time goes:
time: 945 us; the launch traced here: 935 us
  blocking collectives  555 us (59%)
  waiting for transfers between devices  129 us (14%)
  local copies, waits for them, and re-layouts  94 us (10%)
  other arithmetic  86.5 us (9%)
  starting transfers between devices  36 us (4%)
  matrix products  20.1 us (2%)
  between operations  14.9 us (2%)
    all_gather x1, blocking collectives, verify_layer(): piece = lax.all_gather(x_proj, 'dp', axis=0, tiled=True)  184 us
    all_gather x1, blocking collectives, verify_layer(): lax.all_gather(dt_proj, 'dp', axis=0, tiled=True)  160 us
    all_gather x1, blocking collectives, verify_layer(): lax.all_gather(norm_gain, 'mp', axis=0, tiled=True)  141 us
    all_to_all x1, waiting for transfers between devices, on_device(): lax.all_to_all(returned.astype(jnp.bfloat16), 'dp', split_axis=0, concat_...  94.2 us
    psum x1, blocking collectives, verify_layer(): low_full, both = lax.psum((low_sum, both_sum), 'mp')  68.9 us
    all_to_all x1, waiting for transfers between devices, on_device(): lax.all_to_all(pack_rows(hidden, filled, source), 'dp', split_axis=0, con...  23.7 us
    reduce_sum x16, other arithmetic, advance(): output = jnp.sum(state * step_c[:, :, None], axis=1)  19.9 us
  transfers between devices with their start and end apart: 10, of which 3 were waited for; matrix products, arithmetic and copies ran while one was open for 19% of the time, Pallas kernels for 0%

commit v1 on v0

--- a/solution.py
+++ b/solution.py
@@ -86,7 +86,13 @@
         mixed = mixed + conv_weight[offset] * padded[:, offset : offset + drafts, :]
     inputs = jax.nn.silu(mixed).astype(jnp.bfloat16)
     flat_inputs = inputs.reshape(tokens, inner_local)
-    piece = lax.all_gather(x_proj, "dp", axis=0, tiled=True)
+    all_values = lax.all_to_all(
+        jnp.stack([x_proj for _ in range(lax.axis_size("dp"))], 0),
+        axis_name="dp",
+        split_axis=0,
+        concat_axis=0,
+    )
+    piece = jnp.concatenate(all_values, 0)
     columns = flat_inputs
     low_sum = jnp.dot(columns, piece[:, :rank], preferred_element_type=jnp.float32)
     both_sum = jnp.einsum("ks,tk->st", piece[:, rank:], columns, preferred_element_type=jnp.float32)

time: 945 us -> 826 us (0.87)
  blocking collectives: 555 us -> 353 us
  waiting for transfers between devices: 129 us -> 196 us
  starting transfers between devices: 36 us -> 45.8 us
    all_gather x1 -> x0, blocking collectives: 184 us -> none  [verify_layer(): piece = lax.all_gather(x_proj, 'dp', axis=0, tiled=True)]
    all_gather x1, waiting for transfers between devices: 0.01 us -> 66.7 us  [verify_layer(): lax.all_gather(in_x, 'dp', axis=0, tiled=True)]
    psum x1, blocking collectives: 68.9 us -> 42.8 us  [verify_layer(): low_full, both = lax.psum((low_sum, both_sum), 'mp')]
    all_to_all x0 -> x1, starting transfers between devices: none -> 9.52 us  [verify_layer(): lax.all_to_all(jnp.stack([x_proj for _ in range(lax.axis_size('dp'))], 0)...]
  transfers between devices with their start and end apart: 10 -> 11, of which waited for: 3 -> 5; matrix products, arithmetic and copies ran while one was open for 19% -> 22% of each run, Pallas kernels for 0% -> 0%
where the time goes in v1:
time: 826 us; the launch traced here: 814 us
  blocking collectives  353 us (43%)
  waiting for transfers between devices  196 us (24%)
  local copies, waits for them, and re-layouts  94.6 us (11%)
  other arithmetic  86.5 us (10%)
  starting transfers between devices  45.8 us (6%)
  matrix products  22.1 us (3%)
  between operations  14.9 us (2%)
    all_gather x1, blocking collectives, verify_layer(): lax.all_gather(dt_proj, 'dp', axis=0, tiled=True)  168 us
    all_gather x1, blocking collectives, verify_layer(): lax.all_gather(norm_gain, 'mp', axis=0, tiled=True)  143 us
    all_to_all x1, waiting for transfers between devices, on_device(): lax.all_to_all(returned.astype(jnp.bfloat16), 'dp', split_axis=0, concat_...  93 us
    all_gather x1, waiting for transfers between devices, verify_layer(): lax.all_gather(in_x, 'dp', axis=0, tiled=True)  66.7 us
    psum x1, blocking collectives, verify_layer(): low_full, both = lax.psum((low_sum, both_sum), 'mp')  42.8 us
    all_to_all x1, waiting for transfers between devices, on_device(): lax.all_to_all(pack_rows(hidden, filled, source), 'dp', split_axis=0, con...  23.7 us
    reduce_sum x16, other arithmetic, advance(): output = jnp.sum(state * step_c[:, :, None], axis=1)  19.9 us
  transfers between devices with their start and end apart: 11, of which 5 were waited for; matrix products, arithmetic and copies ran while one was open for 22% of the time, Pallas kernels for 0%

profile of v1, /device:TPU:1, one launch (start us, length us, event | category | flops | bytes accessed | tf_op | source)
XLA Modules:
  0.0 813.6 jit_solution(725193732523110120)
XLA Ops:
  11.0 15.1 %all-to-all-start.1 = ((f32[64,1,2]{2,1,0:T(1,128)}), f32[64,1,2]{2,1,0:T(1,128)S(1)}, u32[]{:S(2)}, u32[]{:S(2)}) async-start(f32[64,1,2]{2,1,0:T(1,128)} %copy.94), calls=%async_computation.1 | async-start | bytes 65536 | tf_op jit(solution)/shard_map/all_to_all | solution.py:194
  27.9 8.8 %all-to-all-done.1 = f32[64,1,2]{2,1,0:T(1,128)S(1)} async-done(((f32[64,1,2]{2,1,0:T(1,128)}), f32[64,1,2]{2,1,0:T(1,128)S(1)}, u32[]{:S(2)}, u32[]{:S(2)}) %all-to-all-start.1) | async-done | bytes 544 | tf_op jit(solution)/shard_map/all_to_all | solution.py:194
  36.7 5.5 all-to-all-start.2
  43.8 23.7 %all-to-all-done.2 = bf16[64,16,512]{2,1,0:T(8,128)(2,1)} async-done(((bf16[64,16,512]{2,1,0:T(8,128)(2,1)}), bf16[64,16,512]{2,1,0:T(8,128)(2,1)}, u32[]{:S(2)}, u32[]{:S(2)}) %all-to-all-start.2) | async-done | bytes 1048608 | tf_op jit(solution)/shard_map/all_to_all | solution.py:187
  67.5 2.6 gather_fusion.4
  77.5 3.6 gather_fusion.9
  81.1 7.0 select_select_fusion.1
  88.2 10.0 %all-to-all-start = ((f32[64,19,1024]{2,1,0:T(8,128)}), f32[64,19,1024]{2,1,0:T(8,128)}, u32[]{:S(2)}, u32[]{:S(2)}) async-start(f32[64,19,1024]{2,1,0:T(8,128)} %select_select_fusion.1), calls=%async_computation | async-start | bytes 12582912 | tf_op jit(solution)/shard_map/all_to_all | solution.py:191
  99.0 142.6 %all-gather = bf16[4,1,512]{2,1,0:T(2,128)(2,1)S(1)} all-gather(bf16[1,1,512]{2,1,0:T(2,128)(2,1)S(1)} %reshape.377), channel_id=1, replica_groups=mesh['dp'=64,'mp'=4] {'mp'}, dimensions={0}, use_global_device_ids=true | all-gather | bytes 5120 | tf_op jit(solution)/shard_map/all_gather | solution.py:65
  245.8 66.7 %all-gather.9.cloned.1.call-done = bf16[2048,1024]{1,0:T(8,128)(2,1)} async-done(((bf16[32,1024]{1,0:T(8,128)(2,1)}), bf16[2048,1024]{1,0:T(8,128)(2,1)}) %all-gather.9.cloned.1.call-update) | async-done | bytes 4194320 | tf_op jit(solution)/shard_map/all_gather | solution.py:72
  312.5 5.2 convolution_convert_fusion.1
  319.2 9.5 %all-to-all-start.3 = ((bf16[64,16,160]{2,1,0:T(8,128)(2,1)}), bf16[64,16,160]{2,1,0:T(8,128)(2,1)}, u32[]{:S(2)}, u32[]{:S(2)}) async-start(bf16[64,16,160]{2,1,0:T(8,128)(2,1)} %stack.11), calls=%async_computation.3 | async-start | bytes 1048576 | tf_op jit(solution)/shard_map/all_to_all | solution.py:89
  329.3 5.2 gather_fusion.10
  339.9 2.6 multiply_convert_fusion
  348.5 168.1 %all-gather.1 = bf16[64,2,1024]{2,1,0:T(2,128)(2,1)S(1)} all-gather(bf16[1,2,1024]{2,1,0:T(2,128)(2,1)S(1)} %bitcast.98), channel_id=1, replica_groups=mesh['dp'=64,'mp'=4] {'dp'}, dimensions={0}, use_global_device_ids=true | all-gather | bytes 266240 | tf_op jit(solution)/shard_map/all_gather | solution.py:104
  517.5 4.5 convolution_convert_fusion
  525.5 42.8 %all-reduce.4 = bf16[512,128]{1,0:T(8,128)(2,1)} all-reduce(f32[512,128]{1,0:T(8,128)S(1)} %fusion.12), channel_id=1, replica_groups=mesh['dp'=64,'mp'=4] {'mp'}, use_global_device_ids=true, to_apply=%region_5.8 | all-reduce | flops 65536 | bytes 393216 | tf_op jit(solution)/shard_map/psum | solution.py:99
  568.3 2.3 compare_select_fusion
  570.6 4.6 fusion.3
  578.2 82.8 %while.16 = (s32[]{:T(128)}, f32[32,16,1024]{2,1,0:T(8,128)S(1)}, bf16[32,16,1024]{2,1,0:T(8,128)(2,1)S(1)}, f32[16,32,1024]{2,1,0:T(8,128)}, f32[16,32,1024]{2,...) while((s32[]{:T(128)}, f32[32,16,1024]{2,1,0:T(8,128)S(1)}, ...), condition=%wide.region_9.12_spmd, body=%wide.region_7.11_spmd.sunk | while | flops 3637314 | bytes 9646925 | solution.py:125
  661.1 4.1 fusion.6
  665.8 6.6 fusion.29
  673.9 3.3 gather_fusion.8
  678.0 2.4 gather_fusion.11
  680.3 5.5 fusion
  685.9 4.9 all-to-all-start.4
  691.1 93.0 %all-to-all-done.4 = bf16[64,19,1024]{2,1,0:T(8,128)(2,1)S(1)} async-done(((bf16[64,19,1024]{2,1,0:T(8,128)(2,1)}), bf16[64,19,1024]{2,1,0:T(8,128)(2,1)S(1)}, u32[]{:S(2)}, u32[]{:S(2)}) %all-to-all-start.4) | async-done | bytes 2490400 | tf_op jit(solution)/shard_map/all_to_all | solution.py:218
  784.1 3.4 convert_element_type.91
  787.5 3.5 gather_fusion.12
  794.9 3.0 gather_fusion.7
  800.5 3.7 select_select_fusion.2
  804.1 2.3 add_convert_fusion
  (266 shorter events, 131.7 us)
Async XLA Ops:
  7.2 18.9 %copy-start = (bf16[32,16,512]{2,1,0:T(8,128)(2,1)S(1)}, bf16[32,16,512]{2,1,0:T(8,128)(2,1)}, u32[]{:S(2)}) copy-start(bf16[32,16,512]{2,1,0:T(8,128)(2,1)} %param.23) | copy-start | bytes 1572868
  8.1 19.8 %copy-start.19 = (s32[32]{0:T(128)}, s32[32]{0:T(128)S(1)}, u32[]{:S(2)}) copy-start(s32[32]{0:T(128)S(1)} %get-tuple-element.243) | copy-start | bytes 388
  11.0 25.8 %all-to-all-start.1 = ((f32[64,1,2]{2,1,0:T(1,128)}), f32[64,1,2]{2,1,0:T(1,128)S(1)}, u32[]{:S(2)}, u32[]{:S(2)}) async-start(f32[64,1,2]{2,1,0:T(1,128)} %copy.94), calls=%async_computation.1 | async-start | bytes 65536 | tf_op jit(solution)/shard_map/all_to_all | solution.py:194
  36.7 30.7 %all-to-all-start.2 = ((bf16[64,16,512]{2,1,0:T(8,128)(2,1)}), bf16[64,16,512]{2,1,0:T(8,128)(2,1)}, u32[]{:S(2)}, u32[]{:S(2)}) async-start(bf16[64,16,512]{2,1,0:T(8,128)(2,1)} %select_select_fusion.3), calls=%async_computation.2 | async-start | bytes 2097152 | tf_op jit(solution)/shard_map/all_to_all | solution.py:187
  42.3 30.6 %copy-start.22 = (s32[32]{0:T(128)S(1)}, s32[32]{0:T(128)}, u32[]{:S(2)}) copy-start(s32[32]{0:T(128)} %param.38) | copy-start | bytes 388
  42.3 31.1 %copy-start.8 = (f32[40,16,1024]{2,1,0:T(8,128)S(1)}, f32[40,16,1024]{2,1,0:T(8,128)}, u32[]{:S(2)}) copy-start(f32[40,16,1024]{2,1,0:T(8,128)} %param.35) | copy-start | bytes 7864324
  42.3 199.3 %all-gather.7.cloned.1.call-start = ((), (), s32[]{:S(2)}) async-start(), calls=%async_computation.6 | async-start | bytes 2621440 | tf_op jit(solution)/shard_map/all_gather | solution.py:64
  72.1 240.5 %all-gather.9.cloned.1.call-start = ((), (), s32[]{:S(2)}) async-start(), calls=%async_computation.7 | async-start | bytes 4259840 | tf_op jit(solution)/shard_map/all_gather | solution.py:72
  73.4 2.0 copy-start.2
  75.4 1.6 copy-start.10
  88.2 10.8 %copy-start.18 = (bf16[512]{0:T(512)(128)(2,1)S(1)}, bf16[512]{0:T(512)(128)(2,1)}, u32[]{:S(2)}) copy-start(bf16[512]{0:T(512)(128)(2,1)} %param.24) | copy-start | bytes 3076
  88.2 153.4 %copy-start.13 = (f32[4,1024]{1,0:T(4,128)S(1)}, f32[4,1024]{1,0:T(4,128)}, u32[]{:S(2)}) copy-start(f32[4,1024]{1,0:T(4,128)} %param.27) | copy-start | bytes 49156
  88.2 229.8 %all-to-all-start = ((f32[64,19,1024]{2,1,0:T(8,128)}), f32[64,19,1024]{2,1,0:T(8,128)}, u32[]{:S(2)}, u32[]{:S(2)}) async-start(f32[64,19,1024]{2,1,0:T(8,128)} %select_select_fusion.1), calls=%async_computation | async-start | bytes 12582912 | tf_op jit(solution)/shard_map/all_to_all | solution.py:191
  98.2 419.2 %all-gather.11.cloned.1.call-start = ((), (), s32[]{:S(2)}) async-start(), calls=%async_computation.9 | async-start | bytes 4259840 | tf_op jit(solution)/shard_map/all_gather | solution.py:75
  241.6 2.3 copy-start.9
  319.2 26.6 %all-to-all-start.3 = ((bf16[64,16,160]{2,1,0:T(8,128)(2,1)}), bf16[64,16,160]{2,1,0:T(8,128)(2,1)}, u32[]{:S(2)}, u32[]{:S(2)}) async-start(bf16[64,16,160]{2,1,0:T(8,128)(2,1)} %stack.11), calls=%async_computation.3 | async-start | bytes 1048576 | tf_op jit(solution)/shard_map/all_to_all | solution.py:89
  328.7 246.5 %all-reduce.3.cloned.1.call-start = ((), (), s32[]{:S(2)}) async-start(), calls=%async_computation.8 | async-start | bytes 131072 | tf_op jit(solution)/shard_map/psum | solution.py:99
  336.8 1.7 copy-start.5
  337.1 2.8 copy-start.15
  342.5 6.0 copy-start.16
  342.5 174.9 %copy-start.12 = (f32[16,1024]{1,0:T(8,128)S(1)}, f32[16,1024]{1,0:T(8,128)}, u32[]{:S(2)}) copy-start(f32[16,1024]{1,0:T(8,128)} %param.32) | copy-start | bytes 196612
  342.5 175.0 %copy-start.11 = (bf16[512,2048]{1,0:T(8,128)(2,1)S(1)}, bf16[512,2048]{1,0:T(8,128)(2,1)}, u32[]{:S(2)}) copy-start(bf16[512,2048]{1,0:T(8,128)(2,1)} %fusion.2) | copy-start | bytes 6291460
  347.9 317.9 %all-gather.13.cloned.1.call-start = ((), (), s32[]{:S(2)}) async-start(), calls=%async_computation.10 | async-start | bytes 4259840 | tf_op jit(solution)/shard_map/all_gather | solution.py:148
  348.5 455.7 %reduce-scatter.2.cloned.1.call-start = ((), (), s32[]{:S(2)}) async-start(), calls=%async_computation.11 | async-start | bytes 5242880 | tf_op jit(solution)/shard_map/reduce_scatter | solution.py:151
  522.0 3.2 copy-start.6
  525.1 43.2 %copy-start.21 = (f32[1024]{0:T(1024)S(1)}, f32[1024]{0:T(1024)}, u32[]{:S(2)}) copy-start(f32[1024]{0:T(1024)} %param.31) | copy-start | bytes 12292
  578.2 82.8 %copy-start.17 = (f32[1024]{0:T(1024)S(1)}, f32[1024]{0:T(1024)}, u32[]{:S(2)}) copy-start(f32[1024]{0:T(1024)} %param.33) | copy-start | bytes 12292
  685.9 4.9 copy-start.20
  685.9 98.2 %all-to-all-start.4 = ((bf16[64,19,1024]{2,1,0:T(8,128)(2,1)}), bf16[64,19,1024]{2,1,0:T(8,128)(2,1)S(1)}, u32[]{:S(2)}, u32[]{:S(2)}) async-start(bf16[64,19,1024]{2,1,0:T(8,128)(2,1)} %fusion), calls=%async_computation.5 | async-start | bytes 6291456 | tf_op jit(solution)/shard_map/all_to_all | solution.py:218
  792.7 5.2 copy-start.3
  794.9 5.6 copy-start.7
  800.5 6.0 copy-start.1
  (4 other events, 3.2 us)
Sparse Core Ops, SparseCore 0:
  72.2 72.1 all-gather.6
  147.7 164.7 all-gather.8
  315.8 91.7 all-gather.10
  410.1 39.2 all-reduce.2
  453.1 90.4 all-gather.12
  672.5 87.3 reduce-scatter.1
